TPU v7x, 512 devices: a whole 4x4x16 slice. The times are simulated.
512 devices in a mesh: section: 4 (over y_hi, core), fsdp: 32 (over y_lo, z), ep: 4 (over x).
Axes of the slice: x: 4, y: 4 (y_hi: 2, y_lo: 2; y = y_hi * 2 + y_lo), z: 16, core: 2. Of those that a mesh axis runs over, the one named last changes fastest.
Arguments:
- hidden: bfloat16 [32768, 7168], P(('section', 'fsdp'), 'ep'), may hold values from -6 to 6
- attn_gain: float32 [7168], replicated, may hold values from 0.25 to 1.75
- q_gain: float32 [1536], replicated, may hold values from 0.25 to 1.75
- kv_gain: float32 [512], replicated, may hold values from 0.25 to 1.75
- down_weight: bfloat16 [7168, 2112], P('fsdp', 'ep'), may hold values from -0.0625 to 0.0625
Outputs:
- q_latent: bfloat16 [32768, 1536], P(('section', 'fsdp', 'ep'))
- kv_cache: bfloat16 [32768, 576], P(('section', 'fsdp', 'ep'))
All inputs are finite; a program needn't handle non-finite values.
Results may differ from a plain program's by a relative error of at most 0.0049.
Values may be sent and summed in bfloat16 or wider, within the bound.
A program may use at most 64 MiB of HBM per device.

v0:
```python
import jax
import jax.numpy as jnp
from jax import lax
from jax.sharding import PartitionSpec as P

QL = 1536
KVL = 512
ROPE = 64
LENGTH = 4096
epsilon = 1e-06
rope_base = 10000.0


def from_behind(x, axis, by):
    count = lax.axis_size(axis)
    return lax.ppermute(x, axis, [(i, (i + by) % count) for i in range(count)])


def root_scale(values, gain):
    mean_square = jnp.mean(values * values, axis=-1, keepdims=True)
    return values * lax.rsqrt(mean_square + epsilon) * gain


def rotate(latent, position):
    half_rope = ROPE // 2
    frequency = rope_base ** (-(jnp.arange(half_rope).astype(jnp.float32) / half_rope))
    angle = position.astype(jnp.float32)[:, None] * frequency[None, :]
    first = latent[:, QL + KVL : QL + KVL + half_rope]
    second = latent[:, QL + KVL + half_rope :]
    cosine = jnp.cos(angle)
    sine = jnp.sin(angle)
    return jnp.concatenate([first * cosine - second * sine, second * cosine + first * sine], axis=1)


def on_device(hidden, attn_gain, q_gain, kv_gain, down_weight):
    row_count = hidden.shape[0]
    moved = from_behind(hidden, "section", 1)
    whole = lax.all_gather(moved, "ep", axis=1, tiled=True)
    normed = root_scale(whole.astype(jnp.float32), attn_gain).astype(jnp.bfloat16)
    partial_latent = jnp.dot(
        normed,
        lax.all_gather(down_weight, "fsdp", axis=0, tiled=True),
        preferred_element_type=jnp.float32,
    )
    latent = lax.all_to_all(partial_latent, "ep", split_axis=0, concat_axis=1, tiled=True)
    quarter = latent.shape[0]
    query = root_scale(latent[:, :QL], q_gain).astype(jnp.bfloat16)
    key_value = root_scale(latent[:, QL : QL + KVL], kv_gain)
    row_index = (
        lax.axis_index("fsdp") * row_count + lax.axis_index("ep") * quarter + jnp.arange(quarter)
    )
    position = row_index % LENGTH
    cache = jnp.concatenate([key_value, rotate(latent, position)], axis=1).astype(jnp.bfloat16)
    return (query, cache)


def solution(mesh):
    placed = (P(("section", "fsdp"), "ep"), P(), P(), P(), P("fsdp", "ep"))
    return jax.shard_map(
        on_device,
        mesh=mesh,
        in_specs=placed,
        out_specs=(P(("section", "fsdp", "ep"), None), P(("section", "fsdp", "ep"), None)),
        check_vma=False,
    )
```

profile of v0, /device:TPU:16, one launch (start us, length us, event | category | flops | bytes accessed | tf_op | source)
XLA Modules:
  0.0 287.9 jit_solution(6684082173452654898)
XLA Ops:
  7.2 0.0 all-gather.4.cloned.1.call-start
  7.2 1.9 collective-permute-start
  9.1 14.5 %collective-permute-done = bf16[256,1792]{1,0:T(8,128)(2,1)S(1)} collective-permute-done((bf16[256,1792]{1,0:T(8,128)(2,1)}, bf16[256,1792]{1,0:T(8,128)(2,1)S(1)}, u32[]{:S(2)}, u32[]{:S(2)}) %collective-permute-start) | collective-permute-done | bytes 917536 | tf_op jit(solution)/shard_map/ppermute | solution.py:16
  23.6 0.0 copy-start
  23.6 1.0 copy-done
  24.7 0.0 all-gather.4.cloned.1.call-update
  24.7 0.0 all-gather.6.cloned.1.call-start
  24.7 0.7 all-gather.6.cloned.1.call-update
  25.4 55.2 %all-gather.4.cloned.1.call-done = bf16[256,7168]{1,0:T(8,128)(2,1)} async-done(((bf16[256,1792]{1,0:T(8,128)(2,1)}), bf16[256,7168]{1,0:T(8,128)(2,1)}) %all-gather.4.cloned.1.call-update) | async-done | bytes 3670032 | tf_op jit(solution)/shard_map/all_gather | solution.py:38
  80.6 2.8 fusion
  83.5 147.0 %all-gather.6.cloned.1.call-done = bf16[32,224,528]{1,2,0:T(8,128)(2,1)} async-done(((bf16[1,224,528]{1,2,0:T(8,128)(2,1)}), bf16[32,224,528]{1,2,0:T(8,128)(2,1)}) %all-gather.6.cloned.1.call-update) | async-done | bytes 7569424 | tf_op jit(solution)/shard_map/all_gather | solution.py:42
  230.5 9.9 %copy.16 = bf16[32,224,528]{1,0,2:T(8,128)(2,1)} copy(bf16[32,224,528]{1,2,0:T(8,128)(2,1)} %all-gather.6.cloned.1.call-done) | data formatting | bytes 15138816 | tf_op jit(solution)/shard_map/all_gather | solution.py:42
  240.4 0.0 copy-start.3
  240.4 16.7 %reshape.58 = bf16[7168,528]{0,1:T(8,128)(2,1)} reshape(bf16[32,224,528]{1,0,2:T(8,128)(2,1)} %copy.16) | data formatting | bytes 15138816
  257.0 0.0 copy-done.3
  257.0 0.0 copy-start.1
  257.0 0.0 copy-start.2
  257.0 8.2 %fusion.3 = f32[256,528]{1,0:T(8,128)} fusion(bf16[7168,528]{0,1:T(8,128)(2,1)} %reshape.58, bf16[256,7168]{1,0:T(8,128)(2,1)} %all-gather.4.cloned.1.call-done, f32[7168]{0:T(1024)S(1)} %copy-done.3, f32[256]{0:T(256)S(1)} %add_rsqrt_fusion), kind=kOutput, calls=%fused_computation.5 | convolution fusion | flops 1945108480 | bytes 11809792 | tf_op jit(solution)/shard_map/dot_general | solution.py:40
  265.3 3.8 %all-to-all-start = ((f32[4,64,528]{2,1,0:T(8,128)}), f32[4,64,528]{2,1,0:T(8,128)S(1)}, u32[]{:S(2)}, u32[]{:S(2)}) async-start(f32[4,64,528]{2,1,0:T(8,128)} %bitcast.1), calls=%async_computation | async-start | bytes 1310720 | tf_op jit(solution)/shard_map/all_to_all | solution.py:45
  269.1 8.8 %all-to-all-done = f32[4,64,528]{2,1,0:T(8,128)S(1)} async-done(((f32[4,64,528]{2,1,0:T(8,128)}), f32[4,64,528]{2,1,0:T(8,128)S(1)}, u32[]{:S(2)}, u32[]{:S(2)}) %all-to-all-start) | async-done | bytes 540704 | tf_op jit(solution)/shard_map/all_to_all | solution.py:45
  277.8 0.4 copy.18
  278.3 0.3 all_to_all.17
  278.6 0.1 multiply_reduce_fusion
  278.7 0.1 fusion.17
  278.8 0.1 multiply_reduce_fusion.1
  278.9 0.1 copy.25
  279.0 0.1 copy.24
  279.1 0.2 fusion.12
  279.2 0.1 copy.22
  279.3 0.1 copy.21
  279.5 0.0 copy-done.1
  279.5 0.8 multiply_convert_fusion
  280.3 0.0 copy-done.2
  280.3 0.1 multiply_convert_fusion.1
  280.3 0.7 pad_maximum_fusion
  (5 shorter events, 0.0 us)
Async XLA Ops:
  7.2 73.5 %all-gather.4.cloned.1.call-start = ((), (), s32[]{:S(2)}) async-start(), calls=%async_computation.1 | async-start | bytes 4587520 | tf_op jit(solution)/shard_map/all_gather | solution.py:38
  7.2 16.4 %collective-permute-start = (bf16[256,1792]{1,0:T(8,128)(2,1)}, bf16[256,1792]{1,0:T(8,128)(2,1)S(1)}, u32[]{:S(2)}, u32[]{:S(2)}) collective-permute-start(bf16[256,1792]{1,0:T(8,128)(2,1)} %param.5), channel_id=1, source_target_pairs={{0,128},{128,256},{256,384},{384,0},{1,129},{129,257},{257,385},{3... | collective-permute-start | bytes 2752520 | tf_op jit(solution)/shard_map/ppermute | solution.py:16
  23.6 1.0 copy-start
  24.7 205.8 %all-gather.6.cloned.1.call-start = ((), (), s32[]{:S(2)}) async-start(), calls=%async_computation.2 | async-start | bytes 8921088 | tf_op jit(solution)/shard_map/all_gather | solution.py:42
  240.4 16.7 %copy-start.3 = (f32[7168]{0:T(1024)S(1)}, f32[7168]{0:T(1024)}, u32[]{:S(2)}) copy-start(f32[7168]{0:T(1024)} %param.6) | copy-start | bytes 86020
  257.0 22.4 %copy-start.1 = (f32[1536]{0:T(1024)S(1)}, f32[1536]{0:T(1024)}, u32[]{:S(2)}) copy-start(f32[1536]{0:T(1024)} %param.7) | copy-start | bytes 18436
  257.0 23.2 %copy-start.2 = (f32[512]{0:T(512)S(1)}, f32[512]{0:T(512)}, u32[]{:S(2)}) copy-start(f32[512]{0:T(512)} %param.8) | copy-start | bytes 6148
  265.3 12.6 %all-to-all-start = ((f32[4,64,528]{2,1,0:T(8,128)}), f32[4,64,528]{2,1,0:T(8,128)S(1)}, u32[]{:S(2)}, u32[]{:S(2)}) async-start(f32[4,64,528]{2,1,0:T(8,128)} %bitcast.1), calls=%async_computation | async-start | bytes 1310720 | tf_op jit(solution)/shard_map/all_to_all | solution.py:45
Sparse Core Ops, SparseCore 0:
  24.8 55.7 all-gather.3
  82.7 147.7 all-gather.5
where the time goes:
time: 289 us; the launch traced here: 288 us
  waiting for transfers between devices  226 us (78%)
  local copies, waits for them, and re-layouts  28.7 us (10%)
  between operations  14.1 us (5%)
  matrix products  8.22 us (3%)
  starting transfers between devices  5.8 us (2%)
  other arithmetic  4.86 us (2%)
    all_gather x1, waiting for transfers between devices, on_device(): lax.all_gather(down_weight, 'fsdp', axis=0, tiled=True)  147 us
    all_gather x1, waiting for transfers between devices, on_device(): whole = lax.all_gather(moved, 'ep', axis=1, tiled=True)  55.2 us
    unnamed x11, local copies, waits for them, and re-layouts  17.8 us
    ppermute x1, waiting for transfers between devices, from_behind(): return lax.ppermute(x, axis, [(i, (i + by) % count) for i in range(count)])  14.5 us
    all_gather x1, local copies, waits for them, and re-layouts, on_device(): lax.all_gather(down_weight, 'fsdp', axis=0, tiled=True)  9.89 us
    all_to_all x1, waiting for transfers between devices, on_device(): lax.all_to_all(partial_latent, 'ep', split_axis=0, concat_axis=1, tiled=T...  8.77 us
    dot_general x1, matrix products, on_device(): jnp.dot(normed, lax.all_gather(down_weight, 'fsdp', axis=0, tiled=True),...  8.22 us
  transfers between devices with their start and end apart: 4, of which 4 were waited for; matrix products, arithmetic and copies ran while one was open for 1% of the time, Pallas kernels for 0%

commit v1 on v0

--- a/solution.py
+++ b/solution.py
@@ -1,3 +1,4 @@
+import functools
 import jax
 import jax.numpy as jnp
 from jax import lax
@@ -9,6 +10,15 @@
 LENGTH = 4096
 epsilon = 1e-06
 rope_base = 10000.0
+
+
+def knots_pass(s0, row_axis):
+    return jnp.concatenate(
+        lax.all_to_all(jnp.stack(lax.axis_size(row_axis) * [s0], axis=0), row_axis, 0, 0), axis=1
+    )
+
+
+units_read = functools.partial(knots_pass, row_axis="ep")
 
 
 def from_behind(x, axis, by):
@@ -35,7 +45,7 @@
 def on_device(hidden, attn_gain, q_gain, kv_gain, down_weight):
     row_count = hidden.shape[0]
     moved = from_behind(hidden, "section", 1)
-    whole = lax.all_gather(moved, "ep", axis=1, tiled=True)
+    whole = units_read(moved)
     normed = root_scale(whole.astype(jnp.float32), attn_gain).astype(jnp.bfloat16)
     partial_latent = jnp.dot(
         normed,

time: 289 us -> 221 us (0.76)
  the two profiles are of different devices: /device:TPU:16 before, /device:TPU:8 now
where the time goes in v1:
time: 221 us; the launch traced here: 220 us
  waiting for transfers between devices  91.4 us (41%)
  local copies, waits for them, and re-layouts  47 us (21%)
  blocking collectives  46 us (21%)
  between operations  14.1 us (6%)
  matrix products  9.17 us (4%)
  starting transfers between devices  7.03 us (3%)
  other arithmetic  5.53 us (3%)
    all_gather x1, waiting for transfers between devices, on_device(): lax.all_gather(down_weight, 'fsdp', axis=0, tiled=True)  67.4 us
    all_to_all x1, blocking collectives, knots_pass(): lax.all_to_all(jnp.stack(lax.axis_size(row_axis) * [s0], axis=0), row_axi...  46 us
    unnamed x11, local copies, waits for them, and re-layouts  18.6 us
    convert_element_type x2, local copies, waits for them, and re-layouts, on_device(): whole.astype(jnp.float32)  17.2 us
    ppermute x1, waiting for transfers between devices, from_behind(): return lax.ppermute(x, axis, [(i, (i + by) % count) for i in range(count)])  14.5 us
    all_gather x1, local copies, waits for them, and re-layouts, on_device(): lax.all_gather(down_weight, 'fsdp', axis=0, tiled=True)  9.89 us
    dot_general x1, matrix products, on_device(): jnp.dot(normed, lax.all_gather(down_weight, 'fsdp', axis=0, tiled=True),...  9.17 us
    all_to_all x1, waiting for transfers between devices, on_device(): lax.all_to_all(partial_latent, 'ep', split_axis=0, concat_axis=1, tiled=T...  8.77 us
  transfers between devices with their start and end apart: 3, of which 3 were waited for; matrix products, arithmetic and copies ran while one was open for 10% of the time, Pallas kernels for 0%

profile of v1, /device:TPU:8, one launch (start us, length us, event | category | flops | bytes accessed | tf_op | source)
XLA Modules:
  0.0 220.2 jit_solution(6659669099924211797)
XLA Ops:
  7.2 0.0 all-gather.3.cloned.1.call-start
  7.2 0.7 all-gather.3.cloned.1.call-update
  7.9 1.9 collective-permute-start
  9.8 14.5 %collective-permute-done = bf16[256,1792]{1,0:T(8,128)(2,1)S(1)} collective-permute-done((bf16[256,1792]{1,0:T(8,128)(2,1)}, bf16[256,1792]{1,0:T(8,128)(2,1)S(1)}, u32[]{:S(2)}, u32[]{:S(2)}) %collective-permute-start) | collective-permute-done | bytes 917536 | tf_op jit(solution)/shard_map/ppermute | solution.py:26
  24.3 0.2 stack.2
  24.6 46.0 %all_to_all.21 = bf16[4,256,1792]{2,1,0:T(8,128)(2,1)S(1)} all-to-all(bf16[4,256,1792]{2,1,0:T(8,128)(2,1)S(1)} %stack.2), channel_id=1, replica_groups=mesh['section'=4,'fsdp'=32,'ep'=4] {'ep'}, dimensions={0} | all-to-all | bytes 7340032 | tf_op jit(solution)/shard_map/all_to_all | solution.py:17
  70.5 0.0 copy-start
  70.5 1.8 copy-done
  72.3 0.8 fusion
  73.2 0.1 rsqrt.28
  73.3 2.7 %convert_bitcast_fusion = f32[256,4,1792]{2,0,1:T(8,128)S(1)} fusion(bf16[4,256,1792]{2,1,0:T(8,128)(2,1)} %copy-done), kind=kLoop, calls=%fused_computation.1 | loop fusion | flops 1835008 | bytes 11010048 | tf_op jit(solution)/shard_map/convert_element_type | solution.py:49
  76.0 7.7 %copy.15 = f32[256,4,1792]{2,1,0:T(4,128)} copy(f32[256,4,1792]{2,0,1:T(8,128)S(1)} %convert_bitcast_fusion) | data formatting | bytes 14680064 | tf_op jit(solution)/shard_map/convert_element_type | solution.py:49
  83.7 9.5 %reshape.81 = f32[4,64,7168]{2,1,0:T(8,128)} reshape(f32[256,4,1792]{2,1,0:T(4,128)} %copy.15) | data formatting | bytes 14680064 | tf_op jit(solution)/shard_map/convert_element_type | solution.py:49
  93.2 67.4 %all-gather.3.cloned.1.call-done = bf16[32,224,528]{1,2,0:T(8,128)(2,1)} async-done(((bf16[1,224,528]{1,2,0:T(8,128)(2,1)}), bf16[32,224,528]{1,2,0:T(8,128)(2,1)}) %all-gather.3.cloned.1.call-update) | async-done | bytes 7569424 | tf_op jit(solution)/shard_map/all_gather | solution.py:52
  160.6 9.9 %copy.16 = bf16[32,224,528]{1,0,2:T(8,128)(2,1)} copy(bf16[32,224,528]{1,2,0:T(8,128)(2,1)} %all-gather.3.cloned.1.call-done) | data formatting | bytes 15138816 | tf_op jit(solution)/shard_map/all_gather | solution.py:52
  170.5 0.0 copy-start.3
  170.5 16.6 %reshape.84 = bf16[7168,528,1]{0,1,2:T(8,128)(2,1)} reshape(bf16[32,224,528]{1,0,2:T(8,128)(2,1)} %copy.16) | data formatting | bytes 15138816
  187.1 0.0 copy-done.3
  187.1 0.0 copy-start.2
  187.1 0.0 copy-start.1
  187.1 9.2 %fusion.1 = f32[4,64,528]{2,1,0:T(8,128)} fusion(bf16[7168,528,1]{0,1,2:T(8,128)(2,1)} %reshape.84, f32[4,64,7168]{2,1,0:T(8,128)} %reshape.81, f32[7168]{0:T(1024)S(1)} %copy-done.3, f32[4,64]{1,0:T(4,128)S(1)} %rsqrt.28), kind=kOutput, calls=%fused_computation.4 | convolution fusion | flops 1943273472 | bytes 15479808 | tf_op jit(solution)/shard_map/dot_general | solution.py:50
  196.3 5.1 %all-to-all-start.1 = ((f32[4,64,528]{2,1,0:T(8,128)}), f32[4,64,528]{2,1,0:T(8,128)S(1)}, u32[]{:S(2)}, u32[]{:S(2)}) async-start(f32[4,64,528]{2,1,0:T(8,128)} %fusion.1), calls=%async_computation.1 | async-start | bytes 1310720 | tf_op jit(solution)/shard_map/all_to_all | solution.py:55
  201.4 8.8 %all-to-all-done.1 = f32[4,64,528]{2,1,0:T(8,128)S(1)} async-done(((f32[4,64,528]{2,1,0:T(8,128)}), f32[4,64,528]{2,1,0:T(8,128)S(1)}, u32[]{:S(2)}, u32[]{:S(2)}) %all-to-all-start.1) | async-done | bytes 540704 | tf_op jit(solution)/shard_map/all_to_all | solution.py:55
  210.2 0.4 copy.17
  210.6 0.3 all_to_all.18
  210.9 0.1 multiply_reduce_fusion.1
  211.0 0.1 multiply_reduce_fusion
  211.2 0.1 fusion.14
  211.3 0.1 copy.23
  211.3 0.1 copy.22
  211.4 0.2 fusion.9
  211.6 0.1 copy.20
  211.7 0.1 copy.21
  211.8 0.0 copy-done.2
  211.8 0.1 multiply_convert_fusion.3
  211.9 0.0 copy-done.1
  211.9 0.8 multiply_convert_fusion.2
  212.7 0.7 pad_maximum_fusion
  (5 shorter events, 0.0 us)
Async XLA Ops:
  7.2 153.4 %all-gather.3.cloned.1.call-start = ((), (), s32[]{:S(2)}) async-start(), calls=%async_computation.2 | async-start | bytes 8921088 | tf_op jit(solution)/shard_map/all_gather | solution.py:52
  7.9 16.4 %collective-permute-start = (bf16[256,1792]{1,0:T(8,128)(2,1)}, bf16[256,1792]{1,0:T(8,128)(2,1)S(1)}, u32[]{:S(2)}, u32[]{:S(2)}) collective-permute-start(bf16[256,1792]{1,0:T(8,128)(2,1)} %param.5), channel_id=1, source_target_pairs={{0,128},{128,256},{256,384},{384,0},{1,129},{129,257},{257,385},{3... | collective-permute-start | bytes 2752520 | tf_op jit(solution)/shard_map/ppermute | solution.py:26
  70.5 1.8 copy-start
  170.5 16.6 %copy-start.3 = (f32[7168]{0:T(1024)S(1)}, f32[7168]{0:T(1024)}, u32[]{:S(2)}) copy-start(f32[7168]{0:T(1024)} %param.6) | copy-start | bytes 86020
  187.1 24.7 %copy-start.2 = (f32[512]{0:T(512)S(1)}, f32[512]{0:T(512)}, u32[]{:S(2)}) copy-start(f32[512]{0:T(512)} %param.8) | copy-start | bytes 6148
  187.1 24.8 %copy-start.1 = (f32[1536]{0:T(1024)S(1)}, f32[1536]{0:T(1024)}, u32[]{:S(2)}) copy-start(f32[1536]{0:T(1024)} %param.7) | copy-start | bytes 18436
  196.3 13.9 %all-to-all-start.1 = ((f32[4,64,528]{2,1,0:T(8,128)}), f32[4,64,528]{2,1,0:T(8,128)S(1)}, u32[]{:S(2)}, u32[]{:S(2)}) async-start(f32[4,64,528]{2,1,0:T(8,128)} %fusion.1), calls=%async_computation.1 | async-start | bytes 1310720 | tf_op jit(solution)/shard_map/all_to_all | solution.py:55
Sparse Core Ops, SparseCore 0:
  10.0 150.4 all-gather.2
